TPU v7x, 256 devices: a whole 4x4x8 slice. The times are simulated.
256 devices in a mesh: dp: 16 (over z, core), expert: 16 (over y, x).
Axes of the slice: x: 4, y: 4, z: 8, core: 2. Of those that a mesh axis runs over, the one named last changes fastest.
Arguments:
- tokens: bfloat16 [32768, 2048], P(('dp', 'expert')), may hold values from -6 to 6
- out_grad: bfloat16 [32768, 2048], P(('dp', 'expert')), may hold values from -1.5 to 1.5
- routes: int32 [32768, 2], P(('dp', 'expert')), may hold values from 0 to 15, all different within a row; in each aligned block of 128 rows (0 to 127, 128 to 255, ...) at most 32 rows name the same one
- route_probs: bfloat16 [32768, 2], P(('dp', 'expert')), may hold values from 0.049804688 to 1
- kept_count: int32 [16], P('dp'), may hold values from 512 to 2048, as said below
- gate_weight: bfloat16 [16, 2048, 768], P('expert', 'dp'), may hold values from -0.125 to 0.125
- up_weight: bfloat16 [16, 2048, 768], P('expert', 'dp'), may hold values from -0.125 to 0.125
- down_weight: bfloat16 [16, 2048, 768], P('expert', 'dp'), may hold values from -0.21875 to 0.21875
Outputs:
- token_grad: bfloat16 [32768, 2048], P(('dp', 'expert'))
- prob_grad: bfloat16 [32768, 2], P(('dp', 'expert'))
- weight_grad: bfloat16 [16, 2048, 2304], P('expert', 'dp')
Inputs may be any that keep to these rules, and one draw needn't show every extreme that they name: `routes`: among the rows of one device, no expert is named more than 32 times, and a row names 2 different experts. `kept_count`: rows of a data group whose index within the group is below its count are kept; in every draw some group keeps all its rows and another keeps a quarter of them.
All inputs are finite; a program needn't handle non-finite values.
Results may differ from a plain program's by a relative error of at most 0.018.
Values may be sent and summed in bfloat16 or wider, within the bound.
No kernel may reach another device: no remote copies, remote signals or barrier semaphores. Data moves between devices by JAX's collectives and lax.ppermute only.
A program may use at most 128 MiB of HBM per device.

v0:
```python
import jax
import jax.numpy as jnp
from jax import lax
from jax.sharding import PartitionSpec as P


def contract_rows(left, right):
    return lax.dot_general(
        left, right, (((0,), (0,)), ((), ())), preferred_element_type=jnp.float32
    )


def contract_last(left, right):
    return lax.dot_general(
        left, right, (((1,), (1,)), ((), ())), preferred_element_type=jnp.float32
    )


def per_device(
    tokens, out_grad, routes, route_probs, kept_count, gate_weight, up_weight, down_weight
):
    tok_rows, width = tokens.shape
    top = routes.shape[1]
    experts = lax.axis_size("expert")
    capacity = 2 * tok_rows * top // experts
    slots = experts * capacity
    weights = lax.all_gather(
        jnp.concatenate((gate_weight, up_weight, down_weight), axis=0), "dp", axis=1, tiled=True
    )
    row = lax.axis_index("expert") * tok_rows + jnp.arange(tok_rows, dtype=jnp.int32)
    kept = row < kept_count[0]
    masked = jnp.where(kept[:, None], out_grad, jnp.zeros_like(out_grad))
    flat = routes.reshape(-1)
    onehot = (flat[:, None] == jnp.arange(experts, dtype=jnp.int32)[None, :]).astype(jnp.int32)
    before = jnp.cumsum(onehot, axis=0) - onehot
    position = jnp.sum(before * onehot, axis=1)
    target = (flat * capacity + position).reshape(tok_rows, top)
    slot = jnp.arange(slots, dtype=jnp.int32)[:, None]
    probs = route_probs.astype(jnp.float32)
    match = [slot == target[None, :, k] for k in range(top)]
    placing = (match[0] | match[1]).astype(jnp.bfloat16)
    weighted = (
        jnp.where(match[0], probs[None, :, 0], 0.0) + jnp.where(match[1], probs[None, :, 1], 0.0)
    ).astype(jnp.bfloat16)
    send_rows = jnp.dot(placing, tokens, preferred_element_type=jnp.float32).astype(jnp.bfloat16)
    send_scaled = jnp.dot(weighted, masked, preferred_element_type=jnp.float32).astype(jnp.bfloat16)
    rows_in = lax.all_to_all(send_rows, "expert", split_axis=0, concat_axis=0, tiled=True)
    scaled = lax.all_to_all(send_scaled, "expert", split_axis=0, concat_axis=0, tiled=True)
    pre_gate = jnp.dot(rows_in, weights[0], preferred_element_type=jnp.float32)
    pre_up = jnp.dot(rows_in, weights[1], preferred_element_type=jnp.float32)
    sig = jax.nn.sigmoid(pre_gate)
    act = (pre_gate * sig * pre_up).astype(jnp.bfloat16)
    back_hidden = jnp.dot(scaled, weights[2], preferred_element_type=jnp.float32)
    prob_part = jnp.sum(act.astype(jnp.float32) * back_hidden, axis=1)
    d_gate = (back_hidden * pre_up * sig * (1.0 + pre_gate * (1.0 - sig))).astype(jnp.bfloat16)
    d_up = (back_hidden * pre_gate * sig).astype(jnp.bfloat16)
    weight_grad = lax.psum_scatter(
        jnp.concatenate(
            (
                contract_rows(rows_in, d_gate),
                contract_rows(rows_in, d_up),
                contract_rows(scaled, act),
            ),
            axis=1,
        ).astype(jnp.bfloat16),
        "dp",
        scatter_dimension=0,
        tiled=True,
    )[None]
    route_back = (contract_last(d_gate, weights[0]) + contract_last(d_up, weights[1])).astype(
        jnp.bfloat16
    )
    prob_all = lax.all_gather(
        prob_part.astype(jnp.bfloat16).reshape(experts, capacity), "expert", axis=0, tiled=False
    )
    rows_back = lax.all_to_all(route_back, "expert", split_axis=0, concat_axis=0, tiled=True)
    prob_back = lax.dynamic_index_in_dim(
        prob_all, lax.axis_index("expert"), axis=1, keepdims=False
    ).reshape(slots)
    token_grad = contract_rows(placing, rows_back).astype(jnp.bfloat16)
    prob_grad = jnp.stack(
        [jnp.sum(jnp.where(m, prob_back.astype(jnp.float32)[:, None], 0.0), axis=0) for m in match],
        axis=1,
    )
    prob_grad = (prob_grad / probs).astype(jnp.bfloat16)
    return (token_grad, prob_grad, weight_grad)


def solution(mesh):
    in_specs = (
        P(("dp", "expert"), None),
        P(("dp", "expert"), None),
        P(("dp", "expert"), None),
        P(("dp", "expert"), None),
        P("dp"),
        P("expert", "dp", None),
        P("expert", "dp", None),
        P("expert", "dp", None),
    )
    out_specs = (P(("dp", "expert"), None), P(("dp", "expert"), None), P("expert", "dp", None))
    return jax.shard_map(
        per_device, mesh=mesh, in_specs=in_specs, out_specs=out_specs, check_vma=False
    )
```

profile of v0, /device:TPU:8, one launch (start us, length us, event | category | flops | bytes accessed | tf_op | source)
XLA Modules:
  0.0 198.0 jit_solution(17751260392276215805)
XLA Ops:
  7.2 2.0 %pad_maximum_fusion.1 = bf16[3,128,768]{2,1,0:T(8,128)(2,1)} fusion(bf16[1,128,768]{2,1,0:T(8,128)(2,1)} %param.15, bf16[1,128,768]{2,1,0:T(8,128)(2,1)} %param.14, bf16[1,128,768]{2,1,0:T(8,128)(2,1)} %param.13), kind=kLoop, calls=%fused_computation.20 | loop fusion | flops 589824 | bytes 1179648 | tf_op jit(solution)/shard_map/concatenate | solution.py:28
  11.6 2.0 %convolution_convert_fusion.4 = bf16[512,2048]{1,0:T(8,128)(2,1)} fusion(bf16[128,2048]{1,0:T(8,128)(2,1)S(1)} %copy-done, s32[128]{0:T(128)S(1)} %get-tuple-element.30, s32[128]{0:T(128)S(1)} %get-tuple-element.29), kind=kOutput, calls=%fused_computation.10 | convolution fusion | flops 269680640 | bytes 2622464 | tf_op jit(solution)/shard_map/dot_general | solution.py:45
  13.6 7.5 %all-to-all-start.1 = ((bf16[16,32,2048]{2,1,0:T(8,128)(2,1)}), bf16[16,32,2048]{2,1,0:T(8,128)(2,1)S(1)}, u32[]{:S(2)}, u32[]{:S(2)}) async-start(bf16[16,32,2048]{2,1,0:T(8,128)(2,1)} %bitcast.9), calls=%async_computation.1 | async-start | bytes 4194304 | tf_op jit(solution)/shard_map/all_to_all | solution.py:47
  21.8 2.2 %convolution_convert_fusion.3 = bf16[512,2048]{1,0:T(8,128)(2,1)} fusion(bf16[128,2048]{1,0:T(8,128)(2,1)S(1)} %copy-done.1, pred[128]{0:T(512)(128)(4,1)S(1)} %add_compare_fusion, f32[128]{0:T(128)S(1)} %get-tuple-element.28, f32[128]{0:T(128)S(1)} %get-tuple-element.27, s32[128]{0:T(128)S(1)} %get-tuple-element.30, s32[128]{0:T(128)S(1)} %get-tuple-element.29), kind=kOutput, calls=%fused_computation.9 | convolution fusion | flops 270139392 | bytes 2623616 | tf_op jit(solution)/shard_map/dot_general | solution.py:46
  24.0 27.5 %all-to-all-done.1 = bf16[16,32,2048]{2,1,0:T(8,128)(2,1)S(1)} async-done(((bf16[16,32,2048]{2,1,0:T(8,128)(2,1)}), bf16[16,32,2048]{2,1,0:T(8,128)(2,1)S(1)}, u32[]{:S(2)}, u32[]{:S(2)}) %all-to-all-start.1) | async-done | bytes 2097184 | tf_op jit(solution)/shard_map/all_to_all | solution.py:47
  51.5 5.6 %all-to-all-start = ((bf16[16,32,2048]{2,1,0:T(8,128)(2,1)}), bf16[16,32,2048]{2,1,0:T(8,128)(2,1)}, u32[]{:S(2)}, u32[]{:S(2)}) async-start(bf16[16,32,2048]{2,1,0:T(8,128)(2,1)} %bitcast.6), calls=%async_computation | async-start | bytes 4194304 | tf_op jit(solution)/shard_map/all_to_all | solution.py:48
  57.3 16.9 %all-gather.2.cloned.1.call-done = bf16[3,2048,768]{2,1,0:T(8,128)(2,1)} async-done(((bf16[3,128,768]{2,1,0:T(8,128)(2,1)}), bf16[3,2048,768]{2,1,0:T(8,128)(2,1)}) %all-gather.2.cloned.1.call-update) | async-done | bytes 9437200 | tf_op jit(solution)/shard_map/all_gather | solution.py:27
  74.2 4.8 %fusion.1 = f32[512,768]{1,0:T(8,128)} fusion(bf16[512,2048]{1,0:T(8,128)(2,1)S(1)} %bitcast.67, bf16[3,2048,768]{2,1,0:T(8,128)(2,1)} %all-gather.2.cloned.1.call-done), kind=kOutput, calls=%fused_computation.11 | convolution fusion | flops 1610612736 | bytes 6815744 | tf_op jit(solution)/shard_map/dot_general | solution.py:50
  79.1 4.9 %fusion.3 = f32[512,768]{1,0:T(8,128)} fusion(bf16[512,2048]{1,0:T(8,128)(2,1)S(1)} %bitcast.68, bf16[3,2048,768]{2,1,0:T(8,128)(2,1)} %all-gather.2.cloned.1.call-done), kind=kOutput, calls=%fused_computation.13 | convolution fusion | flops 1610612736 | bytes 6815744 | tf_op jit(solution)/shard_map/dot_general | solution.py:49
  84.7 5.8 %multiply_reduce_fusion = (bf16[512]{0:T(512)(128)(2,1)S(1)}, bf16[512,768]{1,0:T(8,128)(2,1)S(1)}, bf16[512,768]{1,0:T(8,128)(2,1)S(1)}, bf16[512,768]{1,0:T(8,128)(2,1)S(1)}) fusion(f32[512,768]{1,0:T(8,128)} %fusion.1, f32[512,768]{1,0:T(8,128)} %fusion.3, bf16[512,2048]{1,0:T(8,128)(2,1)} %bitcast.7, bf16[3,2048,768]{2,1,0:T(8,128)(2,1)} %all-gather.2.cloned.1.call-done), kind=kOutput, calls=%fused_computation.15 | convolution fusion | flops 1618083328 | bytes 10748928 | tf_op jit(solution)/shard_map/dot_general | solution.py:53
  90.6 3.7 %convolution_convert_fusion = bf16[2048,768]{0,1:T(8,128)(2,1)S(1)} fusion(bf16[512,2048]{1,0:T(8,128)(2,1)} %bitcast.7, bf16[512,768]{1,0:T(8,128)(2,1)S(1)} %get-tuple-element.24), kind=kOutput, calls=%fused_computation.2 | convolution fusion | flops 1612185600 | bytes 6029312 | tf_op jit(solution)/shard_map/dot_general | solution.py:8
  94.3 1.9 convolution_convert_fusion.1
  96.2 1.9 convolution_convert_fusion.2
  98.1 4.7 %pad_maximum_fusion = bf16[2048,2304]{0,1:T(8,128)(2,1)} fusion(bf16[2048,768]{0,1:T(8,128)(2,1)S(1)} %convolution_convert_fusion, bf16[2048,768]{0,1:T(8,128)(2,1)S(1)} %convolution_convert_fusion.1, bf16[2048,768]{0,1:T(8,128)(2,1)S(1)} %convolution_convert_fusion.2), kind=kLoop, calls=%fused_computation | loop fusion | flops 28311552 | bytes 18874368 | tf_op jit(solution)/shard_map/concatenate | solution.py:58
  102.7 12.2 %copy.41 = bf16[2048,2304]{1,0:T(8,128)(2,1)} copy(bf16[2048,2304]{0,1:T(8,128)(2,1)} %pad_maximum_fusion) | data formatting | bytes 18874368
  115.0 1.1 copy-done.5
  116.1 3.7 %fusion.2 = f32[512,2048]{1,0:T(8,128)S(1)} fusion(bf16[512,768]{1,0:T(8,128)(2,1)S(1)} %copy-done.5, bf16[3,2048,768]{2,1,0:T(8,128)(2,1)} %all-gather.2.cloned.1.call-done), kind=kOutput, calls=%fused_computation.12 | convolution fusion | flops 1610612736 | bytes 8126464 | tf_op jit(solution)/shard_map/dot_general | solution.py:14
  119.8 5.0 %add_convert_fusion = bf16[512,2048]{1,0:T(8,128)(2,1)} fusion(f32[512,2048]{1,0:T(8,128)S(1)} %fusion.2, bf16[512,768]{1,0:T(8,128)(2,1)S(1)} %get-tuple-element.26, bf16[3,2048,768]{2,1,0:T(8,128)(2,1)} %all-gather.2.cloned.1.call-done), kind=kOutput, calls=%fused_computation.1 | convolution fusion | flops 1612709888 | bytes 10223616 | tf_op jit(solution)/shard_map/dot_general | solution.py:14
  124.8 6.4 %all-to-all-start.2 = ((bf16[16,32,2048]{2,1,0:T(8,128)(2,1)}), bf16[16,32,2048]{2,1,0:T(8,128)(2,1)S(1)}, u32[]{:S(2)}, u32[]{:S(2)}) async-start(bf16[16,32,2048]{2,1,0:T(8,128)(2,1)} %bitcast.71), calls=%async_computation.2 | async-start | bytes 4194304 | tf_op jit(solution)/shard_map/all_to_all | solution.py:76
  131.4 44.6 %all_gather.7 = bf16[16,16,32]{2,1,0:T(8,128)(2,1)S(1)} all-gather(bf16[1,16,32]{2,1,0:T(8,128)(2,1)S(1)} %convert_element_type.79), channel_id=1, replica_groups=mesh['dp'=16,'expert'=16] {'expert'}, dimensions={0}, use_global_device_ids=true | all-gather | bytes 17408 | tf_op jit(solution)/shard_map/all_gather | solution.py:73
  176.8 1.3 convolution_convert_fusion.5
  178.1 10.7 %reduce-scatter.4.cloned.1.call-done = bf16[128,2304]{1,0:T(8,128)(2,1)} async-done(((bf16[2048,2304]{1,0:T(8,128)(2,1)}), bf16[128,2304]{1,0:T(8,128)(2,1)}) %reduce-scatter.4.cloned.1.call-update) | async-done | bytes 589840
  188.8 1.4 copy.42
  190.1 1.1 copy.40
  (38 shorter events, 4.2 us)
Async XLA Ops:
  7.2 4.4 %copy-start = (bf16[128,2048]{1,0:T(8,128)(2,1)S(1)}, bf16[128,2048]{1,0:T(8,128)(2,1)}, u32[]{:S(2)}) copy-start(bf16[128,2048]{1,0:T(8,128)(2,1)} %param.8) | copy-start | bytes 1572868
  7.2 4.3 %copy-start.2 = (s32[128,2]{0,1:T(2,128)S(1)}, s32[128,2]{0,1:T(2,128)}, u32[]{:S(2)}) copy-start(s32[128,2]{0,1:T(2,128)} %param.10) | copy-start | bytes 3076
  7.2 67.0 %all-gather.2.cloned.1.call-start = ((), (), s32[]{:S(2)}) async-start(), calls=%async_computation.4 | async-start | bytes 10027008 | tf_op jit(solution)/shard_map/all_gather | solution.py:27
  13.6 8.2 %copy-start.3 = (bf16[128,2]{0,1:T(2,128)(2,1)S(1)}, bf16[128,2]{0,1:T(2,128)(2,1)}, u32[]{:S(2)}) copy-start(bf16[128,2]{0,1:T(2,128)(2,1)} %param.11) | copy-start | bytes 1540
  13.6 8.2 %copy-start.1 = (bf16[128,2048]{1,0:T(8,128)(2,1)S(1)}, bf16[128,2048]{1,0:T(8,128)(2,1)}, u32[]{:S(2)}) copy-start(bf16[128,2048]{1,0:T(8,128)(2,1)} %param.9) | copy-start | bytes 1572868
  13.6 37.9 %all-to-all-start.1 = ((bf16[16,32,2048]{2,1,0:T(8,128)(2,1)}), bf16[16,32,2048]{2,1,0:T(8,128)(2,1)S(1)}, u32[]{:S(2)}, u32[]{:S(2)}) async-start(bf16[16,32,2048]{2,1,0:T(8,128)(2,1)} %bitcast.9), calls=%async_computation.1 | async-start | bytes 4194304 | tf_op jit(solution)/shard_map/all_to_all | solution.py:47
  51.5 33.3 %all-to-all-start = ((bf16[16,32,2048]{2,1,0:T(8,128)(2,1)}), bf16[16,32,2048]{2,1,0:T(8,128)(2,1)}, u32[]{:S(2)}, u32[]{:S(2)}) async-start(bf16[16,32,2048]{2,1,0:T(8,128)(2,1)} %bitcast.6), calls=%async_computation | async-start | bytes 4194304 | tf_op jit(solution)/shard_map/all_to_all | solution.py:48
  57.1 131.7 %reduce-scatter.4.cloned.1.call-start = ((), (), s32[]{:S(2)}) async-start(), calls=%async_computation.5 | async-start | bytes 10027008
  90.6 5.6 %copy-start.4 = (bf16[512,768]{1,0:T(8,128)(2,1)}, bf16[512,768]{1,0:T(8,128)(2,1)S(1)}, u32[]{:S(2)}) copy-start(bf16[512,768]{1,0:T(8,128)(2,1)S(1)} %get-tuple-element.25) | copy-start | bytes 2359300
  114.9 1.1 copy-start.5
  124.8 51.9 %all-to-all-start.2 = ((bf16[16,32,2048]{2,1,0:T(8,128)(2,1)}), bf16[16,32,2048]{2,1,0:T(8,128)(2,1)S(1)}, u32[]{:S(2)}, u32[]{:S(2)}) async-start(bf16[16,32,2048]{2,1,0:T(8,128)(2,1)} %bitcast.71), calls=%async_computation.2 | async-start | bytes 4194304 | tf_op jit(solution)/shard_map/all_to_all | solution.py:76
Sparse Core Ops, SparseCore 0:
  10.4 63.7 all-gather.1
  115.1 73.6 reduce-scatter.3
where the time goes:
time: 199 us; the launch traced here: 198 us
  waiting for transfers between devices  55.9 us (28%)
  blocking collectives  44.6 us (22%)
  matrix products  37.2 us (19%)
  starting transfers between devices  19.8 us (10%)
  local copies, waits for them, and re-layouts  17.4 us (9%)
  between operations  14.8 us (7%)
  other arithmetic  8.16 us (4%)
    all_gather x1, blocking collectives, per_device(): lax.all_gather(prob_part.astype(jnp.bfloat16).reshape(experts, capacity),...  44.6 us
    all_to_all x1, waiting for transfers between devices, per_device(): lax.all_to_all(send_rows, 'expert', split_axis=0, concat_axis=0, tiled=True)  27.5 us
    all_gather x1, waiting for transfers between devices, per_device(): lax.all_gather(jnp.concatenate((gate_weight, up_weight, down_weight), axi...  16.9 us
    unnamed x16, local copies, waits for them, and re-layouts  16.6 us
    unnamed x3, waiting for transfers between devices  10.7 us
    dot_general x2, matrix products, contract_last(): lax.dot_general(left, right, (((1,), (1,)), ((), ())), preferred_element_...  8.76 us
    dot_general x4, matrix products, contract_rows(): lax.dot_general(left, right, (((0,), (0,)), ((), ())), preferred_element_...  8.75 us
    all_to_all x1, starting transfers between devices, per_device(): lax.all_to_all(send_rows, 'expert', split_axis=0, concat_axis=0, tiled=True)  7.52 us
  transfers between devices with their start and end apart: 5, of which 4 were waited for; matrix products, arithmetic and copies ran while one was open for 14% of the time, Pallas kernels for 0%

commit v1 on v0

--- a/solution.py
+++ b/solution.py
@@ -24,8 +24,17 @@
     experts = lax.axis_size("expert")
     capacity = 2 * tok_rows * top // experts
     slots = experts * capacity
-    weights = lax.all_gather(
-        jnp.concatenate((gate_weight, up_weight, down_weight), axis=0), "dp", axis=1, tiled=True
+    weights = jnp.concatenate(
+        lax.all_to_all(
+            jnp.stack(
+                [jnp.concatenate((gate_weight, up_weight, down_weight), axis=0)]
+                * lax.axis_size("dp")
+            ),
+            "dp",
+            0,
+            0,
+        ),
+        axis=1,
     )
     row = lax.axis_index("expert") * tok_rows + jnp.arange(tok_rows, dtype=jnp.int32)
     kept = row < kept_count[0]

time: 199 us -> 419 us (2.11)
  waiting for transfers between devices: 55.9 us -> 268 us
  local copies, waits for them, and re-layouts: 17.4 us -> 28.2 us
  starting transfers between devices: 19.8 us -> 27.1 us
  matrix products: 37.2 us -> 32 us
    all_to_all x0 -> x1, waiting for transfers between devices: none -> 204 us  [per_device(): lax.all_to_all(jnp.stack([jnp.concatenate((gate_weight, up_weight, down_w...]
    all_to_all x1, waiting for transfers between devices: 0.82 us -> 19 us  [per_device(): lax.all_to_all(send_scaled, 'expert', split_axis=0, concat_axis=0, tiled=...]
    all_gather x1 -> x0, waiting for transfers between devices: 16.9 us -> none  [per_device(): lax.all_gather(jnp.concatenate((gate_weight, up_weight, down_weight), axi...]
    all_to_all x0 -> x1, starting transfers between devices: none -> 8.74 us  [per_device(): lax.all_to_all(jnp.stack([jnp.concatenate((gate_weight, up_weight, down_w...]
    slice x1 -> x2, local copies, waits for them, and re-layouts: 0.18 us -> 5.55 us  [the longest x1 5.36 us: per_device(): pre_up = jnp.dot(rows_in, weights[1], preferred_element_type=jnp.float32)]
    another operation x1 -> x2, local copies, waits for them, and re-layouts: 0.01 us -> 4.76 us  [the longest x1 4.76 us: per_device(): jnp.stack([jnp.concatenate((gate_weight, up_weight, down_weight), axis=0)...]
    unnamed x3 -> x2, waiting for transfers between devices: 10.7 us -> 15 us
    unnamed x16 -> x32, local copies, waits for them, and re-layouts: 16.6 us -> 17.3 us
  transfers between devices with their start and end apart: 5 -> 5, of which waited for: 4 -> 4; matrix products, arithmetic and copies ran while one was open for 14% -> 5% of each run, Pallas kernels for 0% -> 0%
where the time goes in v1:
time: 419 us
  waiting for transfers between devices  268 us (64%)
  blocking collectives  41.6 us (10%)
  matrix products  32 us (8%)
  local copies, waits for them, and re-layouts  28.2 us (7%)
  starting transfers between devices  27.1 us (6%)
  between operations  14.9 us (4%)
  other arithmetic  6.65 us (2%)
    all_to_all x1, waiting for transfers between devices, per_device(): lax.all_to_all(jnp.stack([jnp.concatenate((gate_weight, up_weight, down_w...  204 us
    all_gather x1, blocking collectives, per_device(): lax.all_gather(prob_part.astype(jnp.bfloat16).reshape(experts, capacity),...  41.6 us
    all_to_all x1, waiting for transfers between devices, per_device(): lax.all_to_all(send_rows, 'expert', split_axis=0, concat_axis=0, tiled=True)  30.3 us
    all_to_all x1, waiting for transfers between devices, per_device(): lax.all_to_all(send_scaled, 'expert', split_axis=0, concat_axis=0, tiled=...  19 us
    unnamed x32, local copies, waits for them, and re-layouts  17.3 us
    unnamed x2, waiting for transfers between devices  15 us
    dot_general x4, matrix products, contract_rows(): lax.dot_general(left, right, (((0,), (0,)), ((), ())), preferred_element_...  9 us
    all_to_all x1, starting transfers between devices, per_device(): lax.all_to_all(jnp.stack([jnp.concatenate((gate_weight, up_weight, down_w...  8.74 us
  transfers between devices with their start and end apart: 5, of which 4 were waited for; matrix products, arithmetic and copies ran while one was open for 5% of the time, Pallas kernels for 0%

profile of v1, /device:TPU:8, one launch (start us, length us, event | category | flops | bytes accessed | tf_op | source)
XLA Modules:
  0.0 418.6 jit_solution(15802599485410447078)
XLA Ops:
  10.2 2.0 convolution_convert_fusion.4
  12.2 7.5 %all-to-all-start.2 = ((bf16[16,32,2048]{2,1,0:T(8,128)(2,1)}), bf16[16,32,2048]{2,1,0:T(8,128)(2,1)S(1)}, u32[]{:S(2)}, u32[]{:S(2)}) async-start(bf16[16,32,2048]{2,1,0:T(8,128)(2,1)} %bitcast.10), calls=%async_computation.2 | async-start | bytes 4194304 | tf_op jit(solution)/shard_map/all_to_all | solution.py:56
  19.8 30.3 %all-to-all-done.2 = bf16[16,32,2048]{2,1,0:T(8,128)(2,1)S(1)} async-done(((bf16[16,32,2048]{2,1,0:T(8,128)(2,1)}), bf16[16,32,2048]{2,1,0:T(8,128)(2,1)S(1)}, u32[]{:S(2)}, u32[]{:S(2)}) %all-to-all-start.2) | async-done | bytes 2097184 | tf_op jit(solution)/shard_map/all_to_all | solution.py:56
  50.1 4.8 %stack.8 = bf16[16,3,128,768]{3,2,1,0:T(8,128)(2,1)} broadcast(bf16[3,128,768]{2,1,0:T(8,128)(2,1)S(1)} %pad_maximum_fusion.1), dimensions={1,2,3} | broadcast | bytes 10027008 | tf_op jit(solution)/shard_map/stack | solution.py:29
  54.9 8.7 %all-to-all-start.1 = ((bf16[16,3,128,768]{3,2,1,0:T(8,128)(2,1)}), bf16[16,3,128,768]{3,2,1,0:T(8,128)(2,1)}, u32[]{:S(2)}, u32[]{:S(2)}) async-start(bf16[16,3,128,768]{3,2,1,0:T(8,128)(2,1)} %stack.8), calls=%async_computation.1 | async-start | bytes 18874368 | tf_op jit(solution)/shard_map/all_to_all | solution.py:28
  64.3 2.1 convolution_convert_fusion.3
  66.5 203.8 %all-to-all-done.1 = bf16[16,3,128,768]{3,2,1,0:T(8,128)(2,1)} async-done(((bf16[16,3,128,768]{3,2,1,0:T(8,128)(2,1)}), bf16[16,3,128,768]{3,2,1,0:T(8,128)(2,1)}, u32[]{:S(2)}, u32[]{:S(2)}) %all-to-all-start.1) | async-done | bytes 9437216 | tf_op jit(solution)/shard_map/all_to_all | solution.py:28
  270.3 5.6 %all-to-all-start = ((bf16[16,32,2048]{2,1,0:T(8,128)(2,1)}), bf16[16,32,2048]{2,1,0:T(8,128)(2,1)}, u32[]{:S(2)}, u32[]{:S(2)}) async-start(bf16[16,32,2048]{2,1,0:T(8,128)(2,1)} %bitcast.6), calls=%async_computation | async-start | bytes 4194304 | tf_op jit(solution)/shard_map/all_to_all | solution.py:57
  276.0 5.4 %fusion.22 = (bf16[1,16,128,768]{3,2,0,1:T(8,128)(2,1)S(1)}, bf16[1,16,128,768]{3,2,0,1:T(8,128)(2,1)S(1)}, bf16[1,16,128,768]{3,2,0,1:T(8,128)(2,1)}) fusion(bf16[3,16,128,768]{3,2,0,1:T(8,128)(2,1)} %bitcast.8), kind=kLoop, calls=%fused_computation.52 | loop fusion | bytes 18874368 | tf_op jit(solution)/shard_map/slice | solution.py:59
  281.4 3.1 fusion.23
  284.5 2.9 fusion.24
  287.5 19.0 %all-to-all-done = bf16[16,32,2048]{2,1,0:T(8,128)(2,1)} async-done(((bf16[16,32,2048]{2,1,0:T(8,128)(2,1)}), bf16[16,32,2048]{2,1,0:T(8,128)(2,1)}, u32[]{:S(2)}, u32[]{:S(2)}) %all-to-all-start) | async-done | bytes 2097184 | tf_op jit(solution)/shard_map/all_to_all | solution.py:57
  306.5 5.8 %multiply_reduce_fusion = (bf16[512]{0:T(512)(128)(2,1)S(1)}, bf16[512,768]{1,0:T(8,128)(2,1)S(1)}, bf16[512,768]{1,0:T(8,128)(2,1)S(1)}, bf16[512,768]{1,0:T(8,128)(2,1)S(1)}) fusion(f32[512,768]{1,0:T(8,128)} %fusion.23, f32[512,768]{1,0:T(8,128)} %fusion.24, bf16[512,2048]{1,0:T(8,128)(2,1)} %bitcast.7, bf16[2048,768]{1,0:T(8,128)(2,1)} %bitcast.66), kind=kOutput, calls=%fused_computation.8 | convolution fusion | flops 1618083328 | bytes 10748928 | tf_op jit(solution)/shard_map/dot_general | solution.py:62
  312.3 4.0 convolution_convert_fusion
  316.3 1.9 convolution_convert_fusion.1
  318.2 1.9 convolution_convert_fusion.2
  320.0 4.4 %pad_maximum_fusion = bf16[2048,2304]{0,1:T(8,128)(2,1)} fusion(bf16[2048,768]{0,1:T(8,128)(2,1)S(1)} %convolution_convert_fusion, bf16[2048,768]{0,1:T(8,128)(2,1)S(1)} %convolution_convert_fusion.1, bf16[2048,768]{0,1:T(8,128)(2,1)S(1)} %convolution_convert_fusion.2), kind=kLoop, calls=%fused_computation | loop fusion | flops 28311552 | bytes 18874368 | tf_op jit(solution)/shard_map/concatenate | solution.py:67
  324.5 12.8 %copy.41 = bf16[2048,2304]{1,0:T(8,128)(2,1)} copy(bf16[2048,2304]{0,1:T(8,128)(2,1)} %pad_maximum_fusion) | data formatting | bytes 18874368
  338.4 3.9 fusion.25
  342.3 3.1 add_convert_fusion
  345.4 5.1 %all-to-all-start.3 = ((bf16[16,32,2048]{2,1,0:T(8,128)(2,1)}), bf16[16,32,2048]{2,1,0:T(8,128)(2,1)S(1)}, u32[]{:S(2)}, u32[]{:S(2)}) async-start(bf16[16,32,2048]{2,1,0:T(8,128)(2,1)} %bitcast.72), calls=%async_computation.3 | async-start | bytes 4194304 | tf_op jit(solution)/shard_map/all_to_all | solution.py:85
  350.6 41.6 %all_gather.3 = bf16[16,16,32]{2,1,0:T(8,128)(2,1)S(1)} all-gather(bf16[1,16,32]{2,1,0:T(8,128)(2,1)S(1)} %convert_element_type.79), channel_id=1, replica_groups=mesh['dp'=16,'expert'=16] {'expert'}, dimensions={0}, use_global_device_ids=true | all-gather | bytes 17408 | tf_op jit(solution)/shard_map/all_gather | solution.py:82
  394.3 15.0 %reduce-scatter.4.cloned.1.call-done = bf16[128,2304]{1,0:T(8,128)(2,1)} async-done(((bf16[2048,2304]{1,0:T(8,128)(2,1)}), bf16[128,2304]{1,0:T(8,128)(2,1)}) %reduce-scatter.4.cloned.1.call-update) | async-done | bytes 589840
  409.3 1.4 copy.42
  (55 shorter events, 7.7 us)
Async XLA Ops:
  7.2 3.0 copy-start
  10.2 9.6 %copy-start.6 = (bf16[1,128,768]{2,1,0:T(8,128)(2,1)S(1)}, bf16[1,128,768]{2,1,0:T(8,128)(2,1)}, u32[]{:S(2)}) copy-start(bf16[1,128,768]{2,1,0:T(8,128)(2,1)} %param.15) | copy-start | bytes 589828
  12.2 7.5 %copy-start.7 = (bf16[1,128,768]{2,1,0:T(8,128)(2,1)S(1)}, bf16[1,128,768]{2,1,0:T(8,128)(2,1)}, u32[]{:S(2)}) copy-start(bf16[1,128,768]{2,1,0:T(8,128)(2,1)} %param.14) | copy-start | bytes 589828
  12.2 7.5 %copy-start.8 = (bf16[1,128,768]{2,1,0:T(8,128)(2,1)S(1)}, bf16[1,128,768]{2,1,0:T(8,128)(2,1)}, u32[]{:S(2)}) copy-start(bf16[1,128,768]{2,1,0:T(8,128)(2,1)} %param.13) | copy-start | bytes 589828
  12.2 37.9 %all-to-all-start.2 = ((bf16[16,32,2048]{2,1,0:T(8,128)(2,1)}), bf16[16,32,2048]{2,1,0:T(8,128)(2,1)S(1)}, u32[]{:S(2)}, u32[]{:S(2)}) async-start(bf16[16,32,2048]{2,1,0:T(8,128)(2,1)} %bitcast.10), calls=%async_computation.2 | async-start | bytes 4194304 | tf_op jit(solution)/shard_map/all_to_all | solution.py:56
  54.9 9.4 %copy-start.9 = (bf16[128,2]{0,1:T(2,128)(2,1)S(1)}, bf16[128,2]{0,1:T(2,128)(2,1)}, u32[]{:S(2)}) copy-start(bf16[128,2]{0,1:T(2,128)(2,1)} %param.11) | copy-start | bytes 1540
  54.9 9.5 %copy-start.5 = (bf16[128,2048]{1,0:T(8,128)(2,1)S(1)}, bf16[128,2048]{1,0:T(8,128)(2,1)}, u32[]{:S(2)}) copy-start(bf16[128,2048]{1,0:T(8,128)(2,1)} %param.9) | copy-start | bytes 1572868
  54.9 215.4 %all-to-all-start.1 = ((bf16[16,3,128,768]{3,2,1,0:T(8,128)(2,1)}), bf16[16,3,128,768]{3,2,1,0:T(8,128)(2,1)}, u32[]{:S(2)}, u32[]{:S(2)}) async-start(bf16[16,3,128,768]{3,2,1,0:T(8,128)(2,1)} %stack.8), calls=%async_computation.1 | async-start | bytes 18874368 | tf_op jit(solution)/shard_map/all_to_all | solution.py:28
  270.3 36.2 %all-to-all-start = ((bf16[16,32,2048]{2,1,0:T(8,128)(2,1)}), bf16[16,32,2048]{2,1,0:T(8,128)(2,1)}, u32[]{:S(2)}, u32[]{:S(2)}) async-start(bf16[16,32,2048]{2,1,0:T(8,128)(2,1)} %bitcast.6), calls=%async_computation | async-start | bytes 4194304 | tf_op jit(solution)/shard_map/all_to_all | solution.py:57
  275.8 133.5 %reduce-scatter.4.cloned.1.call-start = ((), (), s32[]{:S(2)}) async-start(), calls=%async_computation.5 | async-start | bytes 10027008
  281.4 3.1 copy-start.2
  281.4 3.1 copy-start.4
  312.3 4.0 copy-start.10
  312.3 5.9 %copy-start.12 = (bf16[512,768]{1,0:T(8,128)(2,1)}, bf16[512,768]{1,0:T(8,128)(2,1)S(1)}, u32[]{:S(2)}) copy-start(bf16[512,768]{1,0:T(8,128)(2,1)S(1)} %get-tuple-element.28) | copy-start | bytes 2359300
  337.3 1.1 copy-start.13
  338.4 3.9 copy-start.3
  338.4 3.9 copy-start.11
  345.4 47.5 %all-to-all-start.3 = ((bf16[16,32,2048]{2,1,0:T(8,128)(2,1)}), bf16[16,32,2048]{2,1,0:T(8,128)(2,1)S(1)}, u32[]{:S(2)}, u32[]{:S(2)}) async-start(bf16[16,32,2048]{2,1,0:T(8,128)(2,1)} %bitcast.72), calls=%async_computation.3 | async-start | bytes 4194304 | tf_op jit(solution)/shard_map/all_to_all | solution.py:85
  350.5 61.2 %copy-start.1 = (bf16[128,2048]{1,0:T(8,128)(2,1)S(1)}, bf16[128,2048]{1,0:T(8,128)(2,1)}, u32[]{:S(2)}) copy-start(bf16[128,2048]{1,0:T(8,128)(2,1)} %param.8) | copy-start | bytes 1572868
Sparse Core Ops, SparseCore 0:
  337.4 71.7 reduce-scatter.3
